TPU v7x, 32 devices: a whole 2x2x4 slice. The times are simulated.
32 devices in a mesh: groups: 2 (over y), blk: 4 (over z), oct: 2 (over x), sub: 2 (over core).
Axes of the slice: x: 2, y: 2, z: 4, core: 2. Of those that a mesh axis runs over, the one named last changes fastest.
Arguments:
- positions: float32 [3, 65536], P(None, ('groups', 'blk', 'oct', 'sub')), parts along dimension 1, may hold values from 0 to 320
- polarizability: float32 [65536], P(('groups', 'blk', 'oct', 'sub')), parts along dimension 0, may hold values from 0.5 to 1.5
- permanent_field: float32 [3, 65536], P(None, ('groups', 'blk', 'oct', 'sub')), parts along dimension 1, may hold values from -40 to 40
- group_id: int32 [65536], P(('groups', 'blk', 'oct', 'sub')), parts along dimension 0, may hold values from 0 to 10921, never falling along the last dimension, each value on 1 to 6 neighbouring positions
- pair_mask: int32 [512, 9], P(('groups', 'blk', 'oct', 'sub')), parts along dimension 0, may hold values from 0 to 1, as said below
Outputs:
- dipoles: float32 [3, 65536], P(None, ('groups', 'blk', 'oct', 'sub')), parts along dimension 1
- residual: float32 [3, 65536], P(None, ('groups', 'blk', 'oct', 'sub')), parts along dimension 1
There are 2 independent parts, one for each index of `groups`. A program takes and returns all parts, laid end to end along the dimension named above; each array names one. Nothing has to cross between parts.
Inputs may be any that keep to these rules, and one draw needn't show every extreme that they name: `group_id`: never falls from one atom to the next; each value names 1 to 6 consecutive atoms. pair_mask[b, 4] = 1, and pair_mask[b, 4 + o] = pair_mask[(b + o) mod 256, 4 - o].
All inputs are finite; a program needn't handle non-finite values.
Results may differ from a plain program's by a relative error of at most 0.0003.
Values sent between devices are 32-bit elements; how exact they have to be, the bound alone decides.
No kernel may reach another device: no remote copies, remote signals or barrier semaphores. Data moves between devices by JAX's collectives and lax.ppermute only.
A program may use at most 64 MiB of HBM per device.

v0:
```python
import math
import jax
import jax.numpy as jnp
import numpy as np
from jax import lax
from jax.sharding import PartitionSpec as P

BOXES_DEV = 2
BLOCK = 128
ORDER = 5
NODE_PAD = 128
ITERS = 2
side_length = 32.0
layer_gap = 2.5
thole_damp = 0.39
highest = lax.Precision.HIGHEST


def padded(cells, sides, width):
    for axis, dim in sides:
        count = lax.axis_size(axis)
        head = lax.slice_in_dim(cells, 0, width, axis=dim)
        tail = lax.slice_in_dim(cells, cells.shape[dim] - width, cells.shape[dim], axis=dim)
        cells = jnp.concatenate(
            [
                lax.ppermute(tail, axis, [(i, (i + 1) % count) for i in range(count)]),
                cells,
                lax.ppermute(head, axis, [((i + 1) % count, i) for i in range(count)]),
            ],
            axis=dim,
        )
    return cells


def wrap_image(delta, period):
    return delta - period * jnp.floor(delta / period + 0.5)


def split_size(total, limit):
    best = 1
    for factor in range(1, min(total, limit) + 1):
        if total % factor == 0:
            best = factor
    return best


def near_tiles(target, source, moments, keep_tile, length_z):
    delta_x = wrap_image(target[0][:, :, None] - source[0][:, None, :], side_length)
    delta_y = wrap_image(target[1][:, :, None] - source[1][:, None, :], side_length)
    delta_z = wrap_image(target[2][:, :, None] - source[2][:, None, :], length_z)
    keep = (keep_tile[:, None, None] > 0.5) & (target[4][:, :, None] != source[4][:, None, :])
    dist_sq = jnp.where(keep, delta_x * delta_x + delta_y * delta_y + delta_z * delta_z, 1.0)
    inv_three = lax.rsqrt(dist_sq) / dist_sq
    scaled = (
        thole_damp
        * dist_sq
        * jnp.sqrt(dist_sq)
        * lax.rsqrt(target[3][:, :, None] * source[3][:, None, :])
    )
    lam_three = -jnp.expm1(-scaled)
    lam_five = lam_three - scaled * jnp.exp(-scaled)
    coef_five = jnp.where(keep, 3.0 * lam_five * inv_three / dist_sq, 0.0)
    coef_three = jnp.where(keep, lam_three * inv_three, 0.0)
    along = (
        delta_x * moments[0][:, None, :]
        + delta_y * moments[1][:, None, :]
        + delta_z * moments[2][:, None, :]
    )
    weighted = coef_five * along
    field_x = jnp.sum(weighted * delta_x - coef_three * moments[0][:, None, :], axis=2)
    field_y = jnp.sum(weighted * delta_y - coef_three * moments[1][:, None, :], axis=2)
    field_z = jnp.sum(weighted * delta_z - coef_three * moments[2][:, None, :], axis=2)
    return jnp.stack([field_x, field_y, field_z])


def near_total(static_ext, dipole_ext, mask_rows, length_z, atom_count):
    reach = (mask_rows.shape[1] - 1) // 2
    width = reach * BLOCK
    blocks = atom_count // BLOCK
    target = static_ext[:, width : width + atom_count].reshape(5, blocks, BLOCK)
    total = jnp.zeros((3, blocks, BLOCK), static_ext.dtype)
    for offset in range(-reach, reach + 1):
        begin = (reach + offset) * BLOCK
        source = static_ext[:, begin : begin + atom_count].reshape(5, blocks, BLOCK)
        moments = dipole_ext[:, begin : begin + atom_count].reshape(3, blocks, BLOCK)
        keep_tile = mask_rows[:, reach + offset].astype(static_ext.dtype)
        total = total + near_tiles(target, source, moments, keep_tile, length_z)
    return total.reshape(3, atom_count)


def node_tables():
    count = ORDER
    roots = np.cos((2.0 * np.arange(count) + 1.0) * np.pi / (2.0 * count))
    degree = np.arange(count)
    coeff = (
        2.0 / count * np.cos(np.outer(2.0 * np.arange(count) + 1.0, degree) * np.pi / (2.0 * count))
    )
    coeff = np.where(degree[None, :] == 0, 1.0 / count, coeff)
    index = np.arange(NODE_PAD)
    live = index < count**3
    safe = np.where(live, index, 0)
    first = safe // (count * count)
    second = safe // count % count
    third = safe % count
    levels = np.arange(count)[None, :]
    pick_a = (first[:, None] == levels) * live[:, None] * 1.0
    pick_b = (second[:, None] == levels) * 1.0
    pick_c = (third[:, None] == levels) * 1.0
    node_x = 16.0 * (1.0 + roots[first])
    node_y = 16.0 * (1.0 + roots[second])
    node_t = roots[third]
    tables = [coeff, pick_a, pick_b, pick_c, node_x, node_y, node_t]
    return [jnp.asarray(item, jnp.float32) for item in tables]


def interpolation(coords, box_ids, box_height):
    coeff, pick_a, pick_b, pick_c, node_x, node_y, node_t = node_tables()
    scaled_x = coords[0] / 16.0 - 1.0
    scaled_y = coords[1] / 16.0 - 1.0
    scaled_z = (
        2.0 * (coords[2] - box_ids.astype(coords.dtype)[:, None] * box_height) / box_height - 1.0
    )

    def basis(values, picks):
        terms = [jnp.ones_like(values), values]
        for degree in range(2, ORDER):
            terms.append(2.0 * values * terms[-1] - terms[-2])
        stacked = jnp.stack(terms[:ORDER])
        smooth = jnp.einsum("kn,nba->kba", coeff, stacked, precision=highest)
        return jnp.einsum("pk,kba->pba", picks, smooth, precision=highest)

    return basis(scaled_x, pick_a) * basis(scaled_y, pick_b) * basis(scaled_z, pick_c)


def far_block(target_ids, source_ids, weights, slabs, box_height, length_z):
    coeff, pick_a, pick_b, pick_c, node_x, node_y, node_t = node_tables()
    height_t = (
        target_ids.astype(weights.dtype)[:, None] * box_height
        + 0.5 * box_height * (1.0 + node_t)[None, :]
    )
    height_s = (
        source_ids.astype(weights.dtype)[:, None] * box_height
        + 0.5 * box_height * (1.0 + node_t)[None, :]
    )
    delta_x = wrap_image(node_x[:, None] - node_x[None, :], side_length)[None, :, None, :]
    delta_y = wrap_image(node_y[:, None] - node_y[None, :], side_length)[None, :, None, :]
    delta_z = wrap_image(height_t[:, :, None, None] - height_s[None, None, :, :], length_z)
    apart = jnp.abs(target_ids[:, None] // BOXES_DEV - source_ids[None, :] // BOXES_DEV)
    apart = jnp.minimum(apart, slabs - apart)
    keep = (apart >= 1)[:, None, :, None]
    dist_sq = jnp.where(
        keep,
        delta_x * delta_x + delta_y * delta_y + delta_z * delta_z + box_height * box_height,
        1.0,
    )
    inv_three = lax.rsqrt(dist_sq) / dist_sq
    coef_five = jnp.where(keep, 3.0 * inv_three / dist_sq, 0.0)
    coef_three = jnp.where(keep, inv_three, 0.0)
    weight_x = weights[:, 0, :][None, None]
    weight_y = weights[:, 1, :][None, None]
    weight_z = weights[:, 2, :][None, None]
    weighted = coef_five * (delta_x * weight_x + delta_y * weight_y + delta_z * weight_z)
    field_x = jnp.sum(weighted * delta_x - coef_three * weight_x, axis=(2, 3))
    field_y = jnp.sum(weighted * delta_y - coef_three * weight_y, axis=(2, 3))
    field_z = jnp.sum(weighted * delta_z - coef_three * weight_z, axis=(2, 3))
    return jnp.stack([field_x, field_y, field_z], axis=1)


def on_device(positions, polarizability, permanent_field, group_id, pair_mask):
    slabs = lax.axis_size(("blk", "oct", "sub"))
    member = lax.axis_index(("blk", "oct", "sub"))
    atom_count = positions.shape[1]
    length_z = layer_gap * atom_count * slabs / 256.0
    box_height = length_z / (BOXES_DEV * slabs)
    per_box = atom_count // BOXES_DEV
    width = (pair_mask.shape[1] - 1) // 2 * BLOCK
    group_limit = max(1, 32 // BOXES_DEV)
    static = jnp.concatenate(
        [positions, polarizability[None, :], group_id.astype(jnp.float32)[None, :]], axis=0
    )
    static_ext = padded(static, ((("blk", "oct", "sub"), 1),), width)
    own_boxes = member * BOXES_DEV + jnp.arange(BOXES_DEV, dtype=jnp.int32)
    interp = interpolation(positions.reshape(3, BOXES_DEV, per_box), own_boxes, box_height)
    surface = 4.0 * math.pi / 3.0 / (side_length * side_length * length_z)

    def induced(dipoles, total):
        dipole_ext = padded(dipoles, ((("blk", "oct", "sub"), 1),), width)
        near = near_total(static_ext, dipole_ext, pair_mask, length_z, atom_count)
        weights = jnp.einsum(
            "pba,cba->bcp", interp, dipoles.reshape(3, BOXES_DEV, per_box), precision=highest
        )
        piece = lax.all_gather(weights, ("blk", "oct", "sub"), axis=0, tiled=True)
        start = jnp.int32(0)
        count = piece.shape[0]
        size = split_size(count, group_limit)
        grouped = piece.reshape(count // size, size, 3, piece.shape[2])

        def visit(acc, item):
            index, bundle = item
            sources = start + index * size + jnp.arange(size, dtype=jnp.int32)
            return (acc + far_block(own_boxes, sources, bundle, slabs, box_height, length_z), None)

        result, unused = lax.scan(
            visit, jnp.zeros_like(weights), (jnp.arange(count // size, dtype=jnp.int32), grouped)
        )
        far = jnp.einsum("pba,bcp->cba", interp, result, precision=highest).reshape(3, atom_count)
        return near + far - surface * total[:, None]

    def moment(values):
        return lax.psum(jnp.sum(values, axis=1), ("blk", "oct", "sub"))

    def squares(resid, scaled):
        return lax.psum(jnp.sum(resid * scaled), ("blk", "oct", "sub"))

    dipoles = polarizability[None, :] * permanent_field
    residual = induced(dipoles, moment(dipoles))
    precond = polarizability[None, :] * residual
    direction = precond
    norm_now = squares(residual, precond)
    for step in range(ITERS):
        image = direction / polarizability[None, :] - induced(direction, moment(direction))
        rate = norm_now / lax.psum(jnp.sum(direction * image), ("blk", "oct", "sub"))
        dipoles = dipoles + rate * direction
        residual = residual - rate * image
        if step + 1 < ITERS:
            precond = polarizability[None, :] * residual
            norm_next = squares(residual, precond)
            direction = precond + norm_next / norm_now * direction
            norm_now = norm_next
    return (dipoles, residual)


def solution(mesh):
    return jax.shard_map(
        on_device,
        mesh=mesh,
        in_specs=(
            P(None, ("groups", "blk", "oct", "sub")),
            P(("groups", "blk", "oct", "sub")),
            P(None, ("groups", "blk", "oct", "sub")),
            P(("groups", "blk", "oct", "sub")),
            P(("groups", "blk", "oct", "sub"), None),
        ),
        out_specs=(
            P(None, ("groups", "blk", "oct", "sub")),
            P(None, ("groups", "blk", "oct", "sub")),
        ),
        check_vma=False,
    )
```

profile of v0, /device:TPU:0, one launch (start us, length us, event | category | flops | bytes accessed | tf_op | source)
XLA Modules:
  0.0 428.3 jit_solution(15247812564218952183)
XLA Ops:
  2.6 5.0 %collective-permute-start.2 = (f32[5,512]{1,0:T(8,128)S(1)}, f32[5,512]{1,0:T(8,128)S(1)}, u32[]{:S(2)}, u32[]{:S(2)}) collective-permute-start(f32[5,512]{1,0:T(8,128)S(1)} %get-tuple-element.990), channel_id=1, source_target_pairs={{1,0},{2,1},{3,2},{4,3},{5,4},{6,5},{7,6},{8,7},{9,8},{10,9},{11,1... | collective-permute-start | bytes 30728 | tf_op jit(solution)/shard_map/ppermute | solution.py:28
  8.6 4.4 %collective-permute-start.3 = (f32[3,512]{1,0:T(4,128)S(1)}, f32[3,512]{1,0:T(4,128)S(1)}, u32[]{:S(2)}, u32[]{:S(2)}) collective-permute-start(f32[3,512]{1,0:T(4,128)S(1)} %get-tuple-element.1086), channel_id=1, source_target_pairs={{1,0},{2,1},{3,2},{4,3},{5,4},{6,5},{7,6},{8,7},{9,8},{10,9},{11,1... | collective-permute-start | bytes 18440 | tf_op jit(solution)/shard_map/ppermute | solution.py:28
  14.0 29.5 %psum.49 = f32[3]{0:T(128)S(1)} all-reduce(f32[3]{0:T(128)S(1)} %get-tuple-element.927), channel_id=1, replica_groups=mesh['groups'=2,'blk'=4,'oct'=2,'sub'=2] {'blk','oct','sub'}, use_global_device_ids=true, to_apply=%region_33.34 | all-reduce | flops 3 | bytes 24 | tf_op jit(solution)/shard_map/psum | solution.py:210
  52.0 17.8 %all_gather.9 = f32[32,3,128]{2,1,0:T(4,128)S(1)} all-gather(f32[2,3,128]{2,1,0:T(4,128)S(1)} %fusion.782), channel_id=1, replica_groups=mesh['groups'=2,'blk'=4,'oct'=2,'sub'=2] {'blk','oct','sub'}, dimensions={0}, use_global_device_ids=true | all-gather | bytes 52224 | tf_op jit(solution)/shard_map/all_gather | solution.py:192
  69.9 13.5 %while.51 = (s32[]{:T(128)}, f32[2,3,128]{2,0,1:T(2,128)S(1)}, s32[2]{0:T(128)S(1)}, f32[2,16,3,128]{3,1,2,0:T(8,128)S(1)}, s32[]{:T(128)}, /*index=5*/s32[]{:T(...) while((s32[]{:T(128)}, f32[2,3,128]{2,0,1:T(2,128)S(1)}, ...), condition=%wide.region_31.32_spmd.clone.clone.clone.clone, body=%wide.region_27.31_spmd.sunk.clone.clone.clone.clone.sunk | while | flops 16765948 | bytes 2795035 | solution.py:203
  71.8 4.8 %subtract_reduce_fusion.9 = (f32[2,128]{1,0:T(2,128)S(1)}, f32[2,128]{1,0:T(2,128)S(1)}, f32[2,128]{1,0:T(2,128)S(1)}) fusion(f32[16,128]{1,0:T(8,128)S(1)} %get-tuple-element.1216, f32[128,128]{1,0:T(8,128)S(1)} %get-tuple-element.1217, pred[2,16]{1,0:T(4,128)(4,1)S(1)} %fusion.814, f32[16,128]{1,0:T(8,128)S(1)} %broadcast_add_fusion.12, ...), kind=kLoop, calls=%fused_computation.28.clone.1 | loop fusion | flops 15727872 | bytes 1282080 | tf_op jit(solution)/shard_map/while/body/eval_jaxpr/reduce_sum | solution.py:163
  78.5 4.8 %subtract_reduce_fusion.9 = (f32[2,128]{1,0:T(2,128)S(1)}, f32[2,128]{1,0:T(2,128)S(1)}, f32[2,128]{1,0:T(2,128)S(1)}) fusion(f32[16,128]{1,0:T(8,128)S(1)} %get-tuple-element.1216, f32[128,128]{1,0:T(8,128)S(1)} %get-tuple-element.1217, pred[2,16]{1,0:T(4,128)(4,1)S(1)} %fusion.814, f32[16,128]{1,0:T(8,128)S(1)} %broadcast_add_fusion.12, ...), kind=kLoop, calls=%fused_computation.28.clone.1 | loop fusion | flops 15727872 | bytes 1282080 | tf_op jit(solution)/shard_map/while/body/eval_jaxpr/reduce_sum | solution.py:163
  84.2 4.0 fusion.558
  88.2 4.0 fusion.585
  92.2 4.0 fusion.567
  96.2 4.0 fusion.576
  112.2 7.3 %fusion.630 = (f32[16,128]{1,0:T(8,128)S(1)}, f32[16,128]{1,0:T(8,128)S(1)}, f32[16,128]{1,0:T(8,128)S(1)}, f32[16,128]{1,0:T(8,128)S(1)}, f32[16,128]{1,0:T(8,128)S(1)}, /*index=5*/f32[16,128]{1,0:T(8,128)S(1)}) fusion(f32[16,128]{1,0:T(8,128)S(1)} %bitcast.840, f32[16,128]{1,0:T(8,128)S(1)} %bitcast.735, f32[16,128]{1,0:T(8,128)S(1)} %bitcast.931, ...), kind=kLoop, calls=%fused_computation.815 | loop fusion | flops 30920704 | bytes 180256 | tf_op jit(solution)/shard_map/reduce_sum | solution.py:70
  120.7 31.6 %psum.51 = f32[3]{0:T(128)S(1)} all-reduce(f32[3]{0:T(128)S(1)} %get-tuple-element.923), channel_id=1, replica_groups=mesh['groups'=2,'blk'=4,'oct'=2,'sub'=2] {'blk','oct','sub'}, use_global_device_ids=true, to_apply=%region_69.70 | all-reduce | flops 3 | bytes 24 | tf_op jit(solution)/shard_map/psum | solution.py:210
  153.2 4.4 %collective-permute-start.5 = (f32[3,512]{1,0:T(4,128)S(1)}, f32[3,512]{1,0:T(4,128)S(1)}, u32[]{:S(2)}, u32[]{:S(2)}) collective-permute-start(f32[3,512]{1,0:T(4,128)S(1)} %get-tuple-element.1078), channel_id=1, source_target_pairs={{1,0},{2,1},{3,2},{4,3},{5,4},{6,5},{7,6},{8,7},{9,8},{10,9},{11,1... | collective-permute-start | bytes 18440 | tf_op jit(solution)/shard_map/ppermute | solution.py:28
  157.6 17.3 %all_gather.10 = f32[32,3,128]{2,1,0:T(4,128)S(1)} all-gather(f32[2,3,128]{2,1,0:T(4,128)S(1)} %fusion.684), channel_id=1, replica_groups=mesh['groups'=2,'blk'=4,'oct'=2,'sub'=2] {'blk','oct','sub'}, dimensions={0}, use_global_device_ids=true | all-gather | bytes 52224 | tf_op jit(solution)/shard_map/all_gather | solution.py:192
  174.9 13.0 %while.52 = (s32[]{:T(128)}, f32[2,3,128]{2,0,1:T(2,128)S(1)}, s32[2]{0:T(128)S(1)}, f32[2,16,3,128]{3,1,2,0:T(8,128)S(1)}, s32[]{:T(128)}, /*index=5*/s32[]{:T(...) while((s32[]{:T(128)}, f32[2,3,128]{2,0,1:T(2,128)S(1)}, ...), condition=%wide.region_67.68_spmd.clone.clone.clone.clone, body=%wide.region_63.67_spmd.sunk.clone.clone.clone.clone.sunk | while | flops 16765948 | bytes 2795035 | solution.py:203
  176.6 4.8 %subtract_reduce_fusion.10 = (f32[2,128]{1,0:T(2,128)S(1)}, f32[2,128]{1,0:T(2,128)S(1)}, f32[2,128]{1,0:T(2,128)S(1)}) fusion(f32[16,128]{1,0:T(8,128)S(1)} %get-tuple-element.1230, f32[128,128]{1,0:T(8,128)S(1)} %get-tuple-element.1231, pred[2,16]{1,0:T(4,128)(4,1)S(1)} %fusion.817, f32[16,128]{1,0:T(8,128)S(1)} %broadcast_add_fusion.14, ...), kind=kLoop, calls=%fused_computation.82.clone.1 | loop fusion | flops 15727872 | bytes 1282080 | tf_op jit(solution)/shard_map/while/body/eval_jaxpr/reduce_sum | solution.py:163
  183.1 4.8 %subtract_reduce_fusion.10 = (f32[2,128]{1,0:T(2,128)S(1)}, f32[2,128]{1,0:T(2,128)S(1)}, f32[2,128]{1,0:T(2,128)S(1)}) fusion(f32[16,128]{1,0:T(8,128)S(1)} %get-tuple-element.1230, f32[128,128]{1,0:T(8,128)S(1)} %get-tuple-element.1231, pred[2,16]{1,0:T(4,128)(4,1)S(1)} %fusion.817, f32[16,128]{1,0:T(8,128)S(1)} %broadcast_add_fusion.14, ...), kind=kLoop, calls=%fused_computation.82.clone.1 | loop fusion | flops 15727872 | bytes 1282080 | tf_op jit(solution)/shard_map/while/body/eval_jaxpr/reduce_sum | solution.py:163
  200.1 4.0 fusion.557
  216.1 7.3 %fusion.629 = (f32[16,128]{1,0:T(8,128)S(1)}, f32[16,128]{1,0:T(8,128)S(1)}, f32[16,128]{1,0:T(8,128)S(1)}, f32[16,128]{1,0:T(8,128)S(1)}, f32[16,128]{1,0:T(8,128)S(1)}, /*index=5*/f32[16,128]{1,0:T(8,128)S(1)}) fusion(f32[16,128]{1,0:T(8,128)S(1)} %bitcast.872, f32[16,128]{1,0:T(8,128)S(1)} %bitcast.736, f32[16,128]{1,0:T(8,128)S(1)} %bitcast.939, ...), kind=kLoop, calls=%fused_computation.814 | loop fusion | flops 30920704 | bytes 180256 | tf_op jit(solution)/shard_map/reduce_sum | solution.py:70
  225.1 32.1 %all-reduce = (f32[]{:T(128)}, f32[]{:T(128)}) all-reduce(f32[]{:T(128)} %get-tuple-element.870, f32[]{:T(128)} %get-tuple-element.869), channel_id=1, replica_groups=mesh['groups'=2,'blk'=4,'oct'=2,'sub'=2] {'blk','oct','sub'}, use_global_device_ids=true, to_apply=%region_35.36 | all-reduce | flops 2 | bytes 16 | tf_op jit(solution)/shard_map/psum | solution.py:213
  259.1 30.1 %psum.53 = f32[]{:T(128)} all-reduce(f32[]{:T(128)} %fusion.632), channel_id=1, replica_groups=mesh['groups'=2,'blk'=4,'oct'=2,'sub'=2] {'blk','oct','sub'}, use_global_device_ids=true, to_apply=%region_73.74 | all-reduce | flops 1 | bytes 8 | tf_op jit(solution)/shard_map/psum | solution.py:213
  290.6 29.7 %psum.54 = f32[3]{0:T(128)S(1)} all-reduce(f32[3]{0:T(128)S(1)} %get-tuple-element.918), channel_id=1, replica_groups=mesh['groups'=2,'blk'=4,'oct'=2,'sub'=2] {'blk','oct','sub'}, use_global_device_ids=true, to_apply=%region_107.108 | all-reduce | flops 3 | bytes 24 | tf_op jit(solution)/shard_map/psum | solution.py:210
  321.3 4.4 %collective-permute-start.7 = (f32[3,512]{1,0:T(4,128)S(1)}, f32[3,512]{1,0:T(4,128)S(1)}, u32[]{:S(2)}, u32[]{:S(2)}) collective-permute-start(f32[3,512]{1,0:T(4,128)S(1)} %get-tuple-element.1070), channel_id=1, source_target_pairs={{1,0},{2,1},{3,2},{4,3},{5,4},{6,5},{7,6},{8,7},{9,8},{10,9},{11,1... | collective-permute-start | bytes 18440 | tf_op jit(solution)/shard_map/ppermute | solution.py:28
  325.7 17.3 %all_gather.11 = f32[32,3,128]{2,1,0:T(4,128)S(1)} all-gather(f32[2,3,128]{2,1,0:T(4,128)S(1)} %fusion.783), channel_id=1, replica_groups=mesh['groups'=2,'blk'=4,'oct'=2,'sub'=2] {'blk','oct','sub'}, dimensions={0}, use_global_device_ids=true | all-gather | bytes 52224 | tf_op jit(solution)/shard_map/all_gather | solution.py:192
  343.0 13.0 %while.53 = (s32[]{:T(128)}, f32[2,3,128]{2,0,1:T(2,128)S(1)}, s32[2]{0:T(128)S(1)}, f32[2,16,3,128]{3,1,2,0:T(8,128)S(1)}, s32[]{:T(128)}, /*index=5*/s32[]{:T(...) while((s32[]{:T(128)}, f32[2,3,128]{2,0,1:T(2,128)S(1)}, ...), condition=%wide.region_105.106_spmd.clone.clone.clone.clone, body=%wide.region_101.105_spmd.sunk.clone.clone.clone.clone.sunk | while | flops 16765948 | bytes 2795035 | solution.py:203
  344.7 4.8 %subtract_reduce_fusion.11 = (f32[2,128]{1,0:T(2,128)S(1)}, f32[2,128]{1,0:T(2,128)S(1)}, f32[2,128]{1,0:T(2,128)S(1)}) fusion(f32[16,128]{1,0:T(8,128)S(1)} %get-tuple-element.1244, f32[128,128]{1,0:T(8,128)S(1)} %get-tuple-element.1245, pred[2,16]{1,0:T(4,128)(4,1)S(1)} %fusion.820, f32[16,128]{1,0:T(8,128)S(1)} %broadcast_add_fusion.16, ...), kind=kLoop, calls=%fused_computation.136.clone.1 | loop fusion | flops 15727872 | bytes 1282080 | tf_op jit(solution)/shard_map/while/body/eval_jaxpr/reduce_sum | solution.py:163
  351.2 4.8 %subtract_reduce_fusion.11 = (f32[2,128]{1,0:T(2,128)S(1)}, f32[2,128]{1,0:T(2,128)S(1)}, f32[2,128]{1,0:T(2,128)S(1)}) fusion(f32[16,128]{1,0:T(8,128)S(1)} %get-tuple-element.1244, f32[128,128]{1,0:T(8,128)S(1)} %get-tuple-element.1245, pred[2,16]{1,0:T(4,128)(4,1)S(1)} %fusion.820, f32[16,128]{1,0:T(8,128)S(1)} %broadcast_add_fusion.16, ...), kind=kLoop, calls=%fused_computation.136.clone.1 | loop fusion | flops 15727872 | bytes 1282080 | tf_op jit(solution)/shard_map/while/body/eval_jaxpr/reduce_sum | solution.py:163
  368.2 4.0 fusion.574
  376.2 4.0 fusion.610
  384.3 7.3 %fusion.628 = (f32[16,128]{1,0:T(8,128)S(1)}, f32[16,128]{1,0:T(8,128)S(1)}, f32[16,128]{1,0:T(8,128)S(1)}, f32[16,128]{1,0:T(8,128)S(1)}, f32[16,128]{1,0:T(8,128)S(1)}, /*index=5*/f32[16,128]{1,0:T(8,128)S(1)}) fusion(f32[16,128]{1,0:T(8,128)S(1)} %bitcast.862, f32[16,128]{1,0:T(8,128)S(1)} %bitcast.737, f32[16,128]{1,0:T(8,128)S(1)} %bitcast.947, ...), kind=kLoop, calls=%fused_computation.813 | loop fusion | flops 30920704 | bytes 180256 | tf_op jit(solution)/shard_map/reduce_sum | solution.py:70
  393.2 32.0 %psum.55 = f32[]{:T(128)} all-reduce(f32[]{:T(128)} %get-tuple-element.1104), channel_id=1, replica_groups=mesh['groups'=2,'blk'=4,'oct'=2,'sub'=2] {'blk','oct','sub'}, use_global_device_ids=true, to_apply=%region_109.110 | all-reduce | flops 1 | bytes 8 | tf_op jit(solution)/shard_map/psum | solution.py:222
  (190 shorter events, 84.4 us)
Async XLA Ops:
  0.6 45.0 %copy-start.8 = (f32[5,5,1]{1,0,2:T(8,128)S(1)}, f32[5,5,1]{1,0,2:T(8,128)}, u32[]{:S(2)}) copy-start(f32[5,5,1]{1,0,2:T(8,128)} %constant.532) | copy-start | bytes 304
  0.6 45.2 %copy-start.11 = (f32[128,5,1]{0,1,2:T(8,128)S(1)}, f32[128,5,1]{0,1,2:T(8,128)}, u32[]{:S(2)}) copy-start(f32[128,5,1]{0,1,2:T(8,128)} %constant.533) | copy-start | bytes 7684
  2.1 81.8 %collective-permute-start = (f32[5,512]{1,0:T(8,128)S(1)}, f32[5,512]{1,0:T(8,128)S(1)}, u32[]{:S(2)}, u32[]{:S(2)}) collective-permute-start(f32[5,512]{1,0:T(8,128)S(1)} %get-tuple-element.989), channel_id=1, source_target_pairs={{0,1},{1,2},{2,3},{3,4},{4,5},{5,6},{6,7},{7,8},{8,9},{9,10},{10,1... | collective-permute-start | bytes 30728 | tf_op jit(solution)/shard_map/ppermute | solution.py:26
  2.6 81.3 %collective-permute-start.2 = (f32[5,512]{1,0:T(8,128)S(1)}, f32[5,512]{1,0:T(8,128)S(1)}, u32[]{:S(2)}, u32[]{:S(2)}) collective-permute-start(f32[5,512]{1,0:T(8,128)S(1)} %get-tuple-element.990), channel_id=1, source_target_pairs={{1,0},{2,1},{3,2},{4,3},{5,4},{6,5},{7,6},{8,7},{9,8},{10,9},{11,1... | collective-permute-start | bytes 30728 | tf_op jit(solution)/shard_map/ppermute | solution.py:28
  8.6 75.2 %collective-permute-start.1 = (f32[3,512]{1,0:T(4,128)S(1)}, f32[3,512]{1,0:T(4,128)S(1)}, u32[]{:S(2)}, u32[]{:S(2)}) collective-permute-start(f32[3,512]{1,0:T(4,128)S(1)} %get-tuple-element.1085), channel_id=1, source_target_pairs={{0,1},{1,2},{2,3},{3,4},{4,5},{5,6},{6,7},{7,8},{8,9},{9,10},{10,1... | collective-permute-start | bytes 18440 | tf_op jit(solution)/shard_map/ppermute | solution.py:26
  8.6 75.2 %collective-permute-start.3 = (f32[3,512]{1,0:T(4,128)S(1)}, f32[3,512]{1,0:T(4,128)S(1)}, u32[]{:S(2)}, u32[]{:S(2)}) collective-permute-start(f32[3,512]{1,0:T(4,128)S(1)} %get-tuple-element.1086), channel_id=1, source_target_pairs={{1,0},{2,1},{3,2},{4,3},{5,4},{6,5},{7,6},{8,7},{9,8},{10,9},{11,1... | collective-permute-start | bytes 18440 | tf_op jit(solution)/shard_map/ppermute | solution.py:28
  13.1 34.7 %copy-start.10 = (f32[128,5,1]{0,1,2:T(8,128)S(1)}, f32[128,5,1]{0,1,2:T(8,128)}, u32[]{:S(2)}) copy-start(f32[128,5,1]{0,1,2:T(8,128)} %constant.534) | copy-start | bytes 7684
  47.7 1.8 copy-start.9
  51.4 18.4 %copy-start.2 = (f32[128]{0:T(128)S(1)}, f32[128]{0:T(128)}, u32[]{:S(2)}) copy-start(f32[128]{0:T(128)} %constant.2011) | copy-start | bytes 1540
  51.4 18.4 %copy-start.4 = (f32[128]{0:T(128)S(1)}, f32[128]{0:T(128)}, u32[]{:S(2)}) copy-start(f32[128]{0:T(128)} %constant.489.clone..sunk.15) | copy-start | bytes 1540
  51.4 18.4 %copy-start.5 = (f32[128]{0:T(128)S(1)}, f32[128]{0:T(128)}, u32[]{:S(2)}) copy-start(f32[128]{0:T(128)} %constant.2010) | copy-start | bytes 1540
  51.4 18.4 %copy-start.6 = (f32[128]{0:T(128)S(1)}, f32[128]{0:T(128)}, u32[]{:S(2)}) copy-start(f32[128]{0:T(128)} %constant.490.clone..sunk.15) | copy-start | bytes 1540
  51.4 18.4 %copy-start.7 = (f32[128]{0:T(128)S(1)}, f32[128]{0:T(128)}, u32[]{:S(2)}) copy-start(f32[128]{0:T(128)} %constant.2009) | copy-start | bytes 1540
  69.9 13.5 %copy-start = (s32[16,9]{1,0:T(8,128)S(1)}, s32[16,9]{1,0:T(8,128)}, u32[]{:S(2)}) copy-start(s32[16,9]{1,0:T(8,128)} %param.28) | copy-start | bytes 1732
  69.9 13.8 %copy-start.1 = (f32[2048]{0:T(1024)S(1)}, f32[2048]{0:T(1024)}, u32[]{:S(2)}) copy-start(f32[2048]{0:T(1024)} %param.25) | copy-start | bytes 24580
  69.9 14.0 %copy-start.3 = (f32[3,2048]{1,0:T(4,128)S(1)}, f32[3,2048]{1,0:T(4,128)}, u32[]{:S(2)}) copy-start(f32[3,2048]{1,0:T(4,128)} %param.24) | copy-start | bytes 73732
  153.1 34.8 %collective-permute-start.4 = (f32[3,512]{1,0:T(4,128)S(1)}, f32[3,512]{1,0:T(4,128)S(1)}, u32[]{:S(2)}, u32[]{:S(2)}) collective-permute-start(f32[3,512]{1,0:T(4,128)S(1)} %get-tuple-element.1077), channel_id=1, source_target_pairs={{0,1},{1,2},{2,3},{3,4},{4,5},{5,6},{6,7},{7,8},{8,9},{9,10},{10,1... | collective-permute-start | bytes 18440 | tf_op jit(solution)/shard_map/ppermute | solution.py:26
  153.2 34.8 %collective-permute-start.5 = (f32[3,512]{1,0:T(4,128)S(1)}, f32[3,512]{1,0:T(4,128)S(1)}, u32[]{:S(2)}, u32[]{:S(2)}) collective-permute-start(f32[3,512]{1,0:T(4,128)S(1)} %get-tuple-element.1078), channel_id=1, source_target_pairs={{1,0},{2,1},{3,2},{4,3},{5,4},{6,5},{7,6},{8,7},{9,8},{10,9},{11,1... | collective-permute-start | bytes 18440 | tf_op jit(solution)/shard_map/ppermute | solution.py:28
  321.2 34.8 %collective-permute-start.6 = (f32[3,512]{1,0:T(4,128)S(1)}, f32[3,512]{1,0:T(4,128)S(1)}, u32[]{:S(2)}, u32[]{:S(2)}) collective-permute-start(f32[3,512]{1,0:T(4,128)S(1)} %get-tuple-element.1069), channel_id=1, source_target_pairs={{0,1},{1,2},{2,3},{3,4},{4,5},{5,6},{6,7},{7,8},{8,9},{9,10},{10,1... | collective-permute-start | bytes 18440 | tf_op jit(solution)/shard_map/ppermute | solution.py:26
  321.3 34.8 %collective-permute-start.7 = (f32[3,512]{1,0:T(4,128)S(1)}, f32[3,512]{1,0:T(4,128)S(1)}, u32[]{:S(2)}, u32[]{:S(2)}) collective-permute-start(f32[3,512]{1,0:T(4,128)S(1)} %get-tuple-element.1070), channel_id=1, source_target_pairs={{1,0},{2,1},{3,2},{4,3},{5,4},{6,5},{7,6},{8,7},{9,8},{10,9},{11,1... | collective-permute-start | bytes 18440 | tf_op jit(solution)/shard_map/ppermute | solution.py:28
where the time goes:
time: 434 us; the launch traced here: 428 us
  blocking collectives  237 us (55%)
  other arithmetic  145 us (33%)
  starting transfers between devices  19 us (4%)
  matrix products  13.6 us (3%)
  between operations  5.61 us (1%)
    reduce_sum x24, other arithmetic, near_tiles(): jnp.sum(weighted * delta_x - coef_three * moments[0][:, None, :], axis=2)  106 us
    psum x3, blocking collectives, moment(): return lax.psum(jnp.sum(values, axis=1), ('blk', 'oct', 'sub'))  90.8 us
    psum x2, blocking collectives, squares(): return lax.psum(jnp.sum(resid * scaled), ('blk', 'oct', 'sub'))  62.2 us
    all_gather x3, blocking collectives, induced(): piece = lax.all_gather(weights, ('blk', 'oct', 'sub'), axis=0, tiled=True)  52.3 us
    psum x1, blocking collectives, on_device(): lax.psum(jnp.sum(direction * image), ('blk', 'oct', 'sub'))  32 us
    reduce_sum x6, other arithmetic, far_block(): field_x = jnp.sum(weighted * delta_x - coef_three * weight_x, axis=(2, 3))  28.8 us
    ppermute x4, starting transfers between devices, padded(): lax.ppermute(head, axis, [((i + 1) % count, i) for i in range(count)])  18.3 us
  transfers between devices with their start and end apart: 8, of which 0 were waited for; matrix products, arithmetic and copies ran while one was open for 11% of the time, Pallas kernels for 0%

commit v1 on v0

--- a/solution.py
+++ b/solution.py
@@ -207,7 +207,7 @@
         return near + far - surface * total[:, None]
 
     def moment(values):
-        return lax.psum(jnp.sum(values, axis=1), ("blk", "oct", "sub"))
+        return lax.psum(lax.psum(jnp.sum(values, axis=1), ("oct", "sub")), "blk")
 
     def squares(resid, scaled):
         return lax.psum(jnp.sum(resid * scaled), ("blk", "oct", "sub"))

time: 434 us -> 390 us (0.90)
  blocking collectives: 237 us -> 192 us
    psum x3 -> x6, blocking collectives: 90.8 us -> 44.9 us  [moment(): return lax.psum(lax.psum(jnp.sum(values, axis=1), ('oct', 'sub')), 'blk')]
  transfers between devices with their start and end apart: 8 -> 8, of which waited for: 0 -> 0; matrix products, arithmetic and copies ran while one was open for 11% -> 12% of each run, Pallas kernels for 0% -> 0%
where the time goes in v1:
time: 390 us; the launch traced here: 384 us
  blocking collectives  192 us (49%)
  other arithmetic  145 us (37%)
  starting transfers between devices  19 us (5%)
  matrix products  13.6 us (3%)
  between operations  5.71 us (1%)
  local copies, waits for them, and re-layouts  4.59 us (1%)
  loops' own time  4.47 us (1%)
    reduce_sum x24, other arithmetic, near_tiles(): jnp.sum(weighted * delta_x - coef_three * moments[0][:, None, :], axis=2)  106 us
    psum x2, blocking collectives, squares(): return lax.psum(jnp.sum(resid * scaled), ('blk', 'oct', 'sub'))  62.2 us
    all_gather x3, blocking collectives, induced(): piece = lax.all_gather(weights, ('blk', 'oct', 'sub'), axis=0, tiled=True)  53.4 us
    psum x6, blocking collectives, moment(): return lax.psum(lax.psum(jnp.sum(values, axis=1), ('oct', 'sub')), 'blk')  44.9 us
    psum x1, blocking collectives, on_device(): lax.psum(jnp.sum(direction * image), ('blk', 'oct', 'sub'))  31.7 us
    reduce_sum x6, other arithmetic, far_block(): field_x = jnp.sum(weighted * delta_x - coef_three * weight_x, axis=(2, 3))  28.8 us
    ppermute x4, starting transfers between devices, padded(): lax.ppermute(head, axis, [((i + 1) % count, i) for i in range(count)])  18.3 us
  transfers between devices with their start and end apart: 8, of which 0 were waited for; matrix products, arithmetic and copies ran while one was open for 12% of the time, Pallas kernels for 0%

profile of v1, /device:TPU:0, one launch (start us, length us, event | category | flops | bytes accessed | tf_op | source)
XLA Modules:
  0.0 384.1 jit_solution(16571897744576913671)
XLA Ops:
  2.6 5.0 %collective-permute-start.2 = (f32[5,512]{1,0:T(8,128)S(1)}, f32[5,512]{1,0:T(8,128)S(1)}, u32[]{:S(2)}, u32[]{:S(2)}) collective-permute-start(f32[5,512]{1,0:T(8,128)S(1)} %get-tuple-element.990), channel_id=1, source_target_pairs={{1,0},{2,1},{3,2},{4,3},{5,4},{6,5},{7,6},{8,7},{9,8},{10,9},{11,1... | collective-permute-start | bytes 30728 | tf_op jit(solution)/shard_map/ppermute | solution.py:28
  8.6 4.4 %collective-permute-start.3 = (f32[3,512]{1,0:T(4,128)S(1)}, f32[3,512]{1,0:T(4,128)S(1)}, u32[]{:S(2)}, u32[]{:S(2)}) collective-permute-start(f32[3,512]{1,0:T(4,128)S(1)} %get-tuple-element.1086), channel_id=1, source_target_pairs={{1,0},{2,1},{3,2},{4,3},{5,4},{6,5},{7,6},{8,7},{9,8},{10,9},{11,1... | collective-permute-start | bytes 18440 | tf_op jit(solution)/shard_map/ppermute | solution.py:28
  14.0 5.8 %psum.70 = f32[3]{0:T(128)S(1)} all-reduce(f32[3]{0:T(128)S(1)} %get-tuple-element.927), channel_id=1, replica_groups=mesh['groups'=2,'blk'=4,'oct'=2,'sub'=2] {'oct','sub'}, use_global_device_ids=true, to_apply=%region_33.34 | all-reduce | flops 3 | bytes 24 | tf_op jit(solution)/shard_map/psum | solution.py:210
  19.7 8.8 %psum.71 = f32[3]{0:T(128)S(1)} all-reduce(f32[3]{0:T(128)S(1)} %psum.70), channel_id=1, replica_groups=mesh['groups'=2,'blk'=4,'oct'=2,'sub'=2] {'blk'}, use_global_device_ids=true, to_apply=%region_34.35 | all-reduce | flops 3 | bytes 24 | tf_op jit(solution)/shard_map/psum | solution.py:210
  37.1 18.5 %all_gather.9 = f32[32,3,128]{2,1,0:T(4,128)S(1)} all-gather(f32[2,3,128]{2,1,0:T(4,128)S(1)} %fusion.782), channel_id=1, replica_groups=mesh['groups'=2,'blk'=4,'oct'=2,'sub'=2] {'blk','oct','sub'}, dimensions={0}, use_global_device_ids=true | all-gather | bytes 52224 | tf_op jit(solution)/shard_map/all_gather | solution.py:192
  55.7 13.5 %while.51 = (s32[]{:T(128)}, f32[2,3,128]{2,0,1:T(2,128)S(1)}, s32[2]{0:T(128)S(1)}, f32[2,16,3,128]{3,1,2,0:T(8,128)S(1)}, s32[]{:T(128)}, /*index=5*/s32[]{:T(...) while((s32[]{:T(128)}, f32[2,3,128]{2,0,1:T(2,128)S(1)}, ...), condition=%wide.region_31.32_spmd.clone.clone.clone.clone, body=%wide.region_27.31_spmd.sunk.clone.clone.clone.clone.sunk | while | flops 16765948 | bytes 2795035 | solution.py:203
  57.6 4.8 %subtract_reduce_fusion.9 = (f32[2,128]{1,0:T(2,128)S(1)}, f32[2,128]{1,0:T(2,128)S(1)}, f32[2,128]{1,0:T(2,128)S(1)}) fusion(f32[16,128]{1,0:T(8,128)S(1)} %get-tuple-element.1216, f32[128,128]{1,0:T(8,128)S(1)} %get-tuple-element.1217, pred[2,16]{1,0:T(4,128)(4,1)S(1)} %fusion.814, f32[16,128]{1,0:T(8,128)S(1)} %broadcast_add_fusion.12, ...), kind=kLoop, calls=%fused_computation.28.clone.1 | loop fusion | flops 15727872 | bytes 1282080 | tf_op jit(solution)/shard_map/while/body/eval_jaxpr/reduce_sum | solution.py:163
  64.4 4.8 %subtract_reduce_fusion.9 = (f32[2,128]{1,0:T(2,128)S(1)}, f32[2,128]{1,0:T(2,128)S(1)}, f32[2,128]{1,0:T(2,128)S(1)}) fusion(f32[16,128]{1,0:T(8,128)S(1)} %get-tuple-element.1216, f32[128,128]{1,0:T(8,128)S(1)} %get-tuple-element.1217, pred[2,16]{1,0:T(4,128)(4,1)S(1)} %fusion.814, f32[16,128]{1,0:T(8,128)S(1)} %broadcast_add_fusion.12, ...), kind=kLoop, calls=%fused_computation.28.clone.1 | loop fusion | flops 15727872 | bytes 1282080 | tf_op jit(solution)/shard_map/while/body/eval_jaxpr/reduce_sum | solution.py:163
  74.0 4.0 %fusion.585 = (f32[16,128]{1,0:T(8,128)S(1)}, f32[16,128]{1,0:T(8,128)S(1)}, f32[16,128]{1,0:T(8,128)S(1)}) fusion(f32[16,128]{1,0:T(8,128)S(1)} %bitcast.857, f32[16,128]{1,0:T(8,128)S(1)} %bitcast.897, f32[16,128]{1,0:T(8,128)S(1)} %bitcast.925, f32[16,128]{1,0:T(8,128)S(1)} %bitcast.706, f32[16,128]{1,0:T(8,128)S(1)} %bitcast.705, ...), kind=kLoop, calls=%fused_computation.770 | loop fusion | flops 15460352 | bytes 131088 | tf_op jit(solution)/shard_map/reduce_sum | solution.py:70
  82.0 4.0 %fusion.576 = (f32[16,128]{1,0:T(8,128)S(1)}, f32[16,128]{1,0:T(8,128)S(1)}, f32[16,128]{1,0:T(8,128)S(1)}) fusion(f32[16,128]{1,0:T(8,128)S(1)} %bitcast.699, f32[16,128]{1,0:T(8,128)S(1)} %bitcast.789, f32[16,128]{1,0:T(8,128)S(1)} %bitcast.927, f32[16,128]{1,0:T(8,128)S(1)} %bitcast.701, f32[16,128]{1,0:T(8,128)S(1)} %bitcast.700, ...), kind=kLoop, calls=%fused_computation.761 | loop fusion | flops 15460352 | bytes 131088 | tf_op jit(solution)/shard_map/reduce_sum | solution.py:70
  98.1 7.3 %fusion.630 = (f32[16,128]{1,0:T(8,128)S(1)}, f32[16,128]{1,0:T(8,128)S(1)}, f32[16,128]{1,0:T(8,128)S(1)}, f32[16,128]{1,0:T(8,128)S(1)}, f32[16,128]{1,0:T(8,128)S(1)}, /*index=5*/f32[16,128]{1,0:T(8,128)S(1)}) fusion(f32[16,128]{1,0:T(8,128)S(1)} %bitcast.840, f32[16,128]{1,0:T(8,128)S(1)} %bitcast.735, f32[16,128]{1,0:T(8,128)S(1)} %bitcast.931, ...), kind=kLoop, calls=%fused_computation.815 | loop fusion | flops 30920704 | bytes 180256 | tf_op jit(solution)/shard_map/reduce_sum | solution.py:70
  106.5 6.9 %psum.73 = f32[3]{0:T(128)S(1)} all-reduce(f32[3]{0:T(128)S(1)} %get-tuple-element.923), channel_id=1, replica_groups=mesh['groups'=2,'blk'=4,'oct'=2,'sub'=2] {'oct','sub'}, use_global_device_ids=true, to_apply=%region_70.71 | all-reduce | flops 3 | bytes 24 | tf_op jit(solution)/shard_map/psum | solution.py:210
  113.3 9.1 %psum.74 = f32[3]{0:T(128)S(1)} all-reduce(f32[3]{0:T(128)S(1)} %psum.73), channel_id=1, replica_groups=mesh['groups'=2,'blk'=4,'oct'=2,'sub'=2] {'blk'}, use_global_device_ids=true, to_apply=%region_71.72 | all-reduce | flops 3 | bytes 24 | tf_op jit(solution)/shard_map/psum | solution.py:210
  123.3 4.4 %collective-permute-start.5 = (f32[3,512]{1,0:T(4,128)S(1)}, f32[3,512]{1,0:T(4,128)S(1)}, u32[]{:S(2)}, u32[]{:S(2)}) collective-permute-start(f32[3,512]{1,0:T(4,128)S(1)} %get-tuple-element.1078), channel_id=1, source_target_pairs={{1,0},{2,1},{3,2},{4,3},{5,4},{6,5},{7,6},{8,7},{9,8},{10,9},{11,1... | collective-permute-start | bytes 18440 | tf_op jit(solution)/shard_map/ppermute | solution.py:28
  127.8 17.3 %all_gather.10 = f32[32,3,128]{2,1,0:T(4,128)S(1)} all-gather(f32[2,3,128]{2,1,0:T(4,128)S(1)} %fusion.684), channel_id=1, replica_groups=mesh['groups'=2,'blk'=4,'oct'=2,'sub'=2] {'blk','oct','sub'}, dimensions={0}, use_global_device_ids=true | all-gather | bytes 52224 | tf_op jit(solution)/shard_map/all_gather | solution.py:192
  145.1 13.5 %while.52 = (s32[]{:T(128)}, f32[2,3,128]{2,0,1:T(2,128)S(1)}, s32[2]{0:T(128)S(1)}, f32[2,16,3,128]{3,1,2,0:T(8,128)S(1)}, s32[]{:T(128)}, /*index=5*/s32[]{:T(...) while((s32[]{:T(128)}, f32[2,3,128]{2,0,1:T(2,128)S(1)}, ...), condition=%wide.region_68.69_spmd.clone.clone.clone.clone, body=%wide.region_64.68_spmd.sunk.clone.clone.clone.clone.sunk | while | flops 16765948 | bytes 2795035 | solution.py:203
  147.0 4.8 %subtract_reduce_fusion.10 = (f32[2,128]{1,0:T(2,128)S(1)}, f32[2,128]{1,0:T(2,128)S(1)}, f32[2,128]{1,0:T(2,128)S(1)}) fusion(f32[16,128]{1,0:T(8,128)S(1)} %get-tuple-element.1230, f32[128,128]{1,0:T(8,128)S(1)} %get-tuple-element.1231, pred[2,16]{1,0:T(4,128)(4,1)S(1)} %fusion.817, f32[16,128]{1,0:T(8,128)S(1)} %broadcast_add_fusion.14, ...), kind=kLoop, calls=%fused_computation.82.clone.1 | loop fusion | flops 15727872 | bytes 1282080 | tf_op jit(solution)/shard_map/while/body/eval_jaxpr/reduce_sum | solution.py:163
  153.7 4.8 %subtract_reduce_fusion.10 = (f32[2,128]{1,0:T(2,128)S(1)}, f32[2,128]{1,0:T(2,128)S(1)}, f32[2,128]{1,0:T(2,128)S(1)}) fusion(f32[16,128]{1,0:T(8,128)S(1)} %get-tuple-element.1230, f32[128,128]{1,0:T(8,128)S(1)} %get-tuple-element.1231, pred[2,16]{1,0:T(4,128)(4,1)S(1)} %fusion.817, f32[16,128]{1,0:T(8,128)S(1)} %broadcast_add_fusion.14, ...), kind=kLoop, calls=%fused_computation.82.clone.1 | loop fusion | flops 15727872 | bytes 1282080 | tf_op jit(solution)/shard_map/while/body/eval_jaxpr/reduce_sum | solution.py:163
  186.7 7.3 %fusion.629 = (f32[16,128]{1,0:T(8,128)S(1)}, f32[16,128]{1,0:T(8,128)S(1)}, f32[16,128]{1,0:T(8,128)S(1)}, f32[16,128]{1,0:T(8,128)S(1)}, f32[16,128]{1,0:T(8,128)S(1)}, /*index=5*/f32[16,128]{1,0:T(8,128)S(1)}) fusion(f32[16,128]{1,0:T(8,128)S(1)} %bitcast.872, f32[16,128]{1,0:T(8,128)S(1)} %bitcast.736, f32[16,128]{1,0:T(8,128)S(1)} %bitcast.939, ...), kind=kLoop, calls=%fused_computation.814 | loop fusion | flops 30920704 | bytes 180256 | tf_op jit(solution)/shard_map/reduce_sum | solution.py:70
  195.7 32.1 %all-reduce = (f32[]{:T(128)}, f32[]{:T(128)}) all-reduce(f32[]{:T(128)} %get-tuple-element.870, f32[]{:T(128)} %get-tuple-element.869), channel_id=1, replica_groups=mesh['groups'=2,'blk'=4,'oct'=2,'sub'=2] {'blk','oct','sub'}, use_global_device_ids=true, to_apply=%region_36.37 | all-reduce | flops 2 | bytes 16 | tf_op jit(solution)/shard_map/psum | solution.py:213
  229.8 30.1 %psum.76 = f32[]{:T(128)} all-reduce(f32[]{:T(128)} %fusion.632), channel_id=1, replica_groups=mesh['groups'=2,'blk'=4,'oct'=2,'sub'=2] {'blk','oct','sub'}, use_global_device_ids=true, to_apply=%region_75.76 | all-reduce | flops 1 | bytes 8 | tf_op jit(solution)/shard_map/psum | solution.py:213
  261.4 5.8 %psum.77 = f32[3]{0:T(128)S(1)} all-reduce(f32[3]{0:T(128)S(1)} %get-tuple-element.918), channel_id=1, replica_groups=mesh['groups'=2,'blk'=4,'oct'=2,'sub'=2] {'oct','sub'}, use_global_device_ids=true, to_apply=%region_109.110 | all-reduce | flops 3 | bytes 24 | tf_op jit(solution)/shard_map/psum | solution.py:210
  267.2 8.6 %psum.78 = f32[3]{0:T(128)S(1)} all-reduce(f32[3]{0:T(128)S(1)} %psum.77), channel_id=1, replica_groups=mesh['groups'=2,'blk'=4,'oct'=2,'sub'=2] {'blk'}, use_global_device_ids=true, to_apply=%region_110.111 | all-reduce | flops 3 | bytes 24 | tf_op jit(solution)/shard_map/psum | solution.py:210
  276.7 4.4 %collective-permute-start.7 = (f32[3,512]{1,0:T(4,128)S(1)}, f32[3,512]{1,0:T(4,128)S(1)}, u32[]{:S(2)}, u32[]{:S(2)}) collective-permute-start(f32[3,512]{1,0:T(4,128)S(1)} %get-tuple-element.1070), channel_id=1, source_target_pairs={{1,0},{2,1},{3,2},{4,3},{5,4},{6,5},{7,6},{8,7},{9,8},{10,9},{11,1... | collective-permute-start | bytes 18440 | tf_op jit(solution)/shard_map/ppermute | solution.py:28
  281.1 17.6 %all_gather.11 = f32[32,3,128]{2,1,0:T(4,128)S(1)} all-gather(f32[2,3,128]{2,1,0:T(4,128)S(1)} %fusion.783), channel_id=1, replica_groups=mesh['groups'=2,'blk'=4,'oct'=2,'sub'=2] {'blk','oct','sub'}, dimensions={0}, use_global_device_ids=true | all-gather | bytes 52224 | tf_op jit(solution)/shard_map/all_gather | solution.py:192
  298.7 13.5 %while.53 = (s32[]{:T(128)}, f32[2,3,128]{2,0,1:T(2,128)S(1)}, s32[2]{0:T(128)S(1)}, f32[2,16,3,128]{3,1,2,0:T(8,128)S(1)}, s32[]{:T(128)}, /*index=5*/s32[]{:T(...) while((s32[]{:T(128)}, f32[2,3,128]{2,0,1:T(2,128)S(1)}, ...), condition=%wide.region_107.108_spmd.clone.clone.clone.clone, body=%wide.region_103.107_spmd.sunk.clone.clone.clone.clone.sunk | while | flops 16765948 | bytes 2795035 | solution.py:203
  300.6 4.8 %subtract_reduce_fusion.11 = (f32[2,128]{1,0:T(2,128)S(1)}, f32[2,128]{1,0:T(2,128)S(1)}, f32[2,128]{1,0:T(2,128)S(1)}) fusion(f32[16,128]{1,0:T(8,128)S(1)} %get-tuple-element.1244, f32[128,128]{1,0:T(8,128)S(1)} %get-tuple-element.1245, pred[2,16]{1,0:T(4,128)(4,1)S(1)} %fusion.820, f32[16,128]{1,0:T(8,128)S(1)} %broadcast_add_fusion.16, ...), kind=kLoop, calls=%fused_computation.136.clone.1 | loop fusion | flops 15727872 | bytes 1282080 | tf_op jit(solution)/shard_map/while/body/eval_jaxpr/reduce_sum | solution.py:163
  307.4 4.8 %subtract_reduce_fusion.11 = (f32[2,128]{1,0:T(2,128)S(1)}, f32[2,128]{1,0:T(2,128)S(1)}, f32[2,128]{1,0:T(2,128)S(1)}) fusion(f32[16,128]{1,0:T(8,128)S(1)} %get-tuple-element.1244, f32[128,128]{1,0:T(8,128)S(1)} %get-tuple-element.1245, pred[2,16]{1,0:T(4,128)(4,1)S(1)} %fusion.820, f32[16,128]{1,0:T(8,128)S(1)} %broadcast_add_fusion.16, ...), kind=kLoop, calls=%fused_computation.136.clone.1 | loop fusion | flops 15727872 | bytes 1282080 | tf_op jit(solution)/shard_map/while/body/eval_jaxpr/reduce_sum | solution.py:163
  324.4 4.0 %fusion.574 = (f32[16,128]{1,0:T(8,128)S(1)}, f32[16,128]{1,0:T(8,128)S(1)}, f32[16,128]{1,0:T(8,128)S(1)}) fusion(f32[16,128]{1,0:T(8,128)S(1)} %bitcast.711, f32[16,128]{1,0:T(8,128)S(1)} %bitcast.791, f32[16,128]{1,0:T(8,128)S(1)} %bitcast.943, f32[16,128]{1,0:T(8,128)S(1)} %bitcast.713, f32[16,128]{1,0:T(8,128)S(1)} %bitcast.712, ...), kind=kLoop, calls=%fused_computation.759 | loop fusion | flops 15460352 | bytes 131088 | tf_op jit(solution)/shard_map/reduce_sum | solution.py:70
  332.4 4.0 %fusion.610 = (f32[16,128]{1,0:T(8,128)S(1)}, f32[16,128]{1,0:T(8,128)S(1)}, f32[16,128]{1,0:T(8,128)S(1)}) fusion(f32[16,128]{1,0:T(8,128)S(1)} %bitcast.879, f32[16,128]{1,0:T(8,128)S(1)} %bitcast.764, f32[16,128]{1,0:T(8,128)S(1)} %bitcast.945, f32[16,128]{1,0:T(8,128)S(1)} %bitcast.881, f32[16,128]{1,0:T(8,128)S(1)} %bitcast.880, ...), kind=kLoop, calls=%fused_computation.795 | loop fusion | flops 15460352 | bytes 131088 | tf_op jit(solution)/shard_map/reduce_sum | solution.py:70
  340.4 7.3 %fusion.628 = (f32[16,128]{1,0:T(8,128)S(1)}, f32[16,128]{1,0:T(8,128)S(1)}, f32[16,128]{1,0:T(8,128)S(1)}, f32[16,128]{1,0:T(8,128)S(1)}, f32[16,128]{1,0:T(8,128)S(1)}, /*index=5*/f32[16,128]{1,0:T(8,128)S(1)}) fusion(f32[16,128]{1,0:T(8,128)S(1)} %bitcast.862, f32[16,128]{1,0:T(8,128)S(1)} %bitcast.737, f32[16,128]{1,0:T(8,128)S(1)} %bitcast.947, ...), kind=kLoop, calls=%fused_computation.813 | loop fusion | flops 30920704 | bytes 180256 | tf_op jit(solution)/shard_map/reduce_sum | solution.py:70
  349.4 31.7 %psum.79 = f32[]{:T(128)} all-reduce(f32[]{:T(128)} %get-tuple-element.1104), channel_id=1, replica_groups=mesh['groups'=2,'blk'=4,'oct'=2,'sub'=2] {'blk','oct','sub'}, use_global_device_ids=true, to_apply=%region_112.113 | all-reduce | flops 1 | bytes 8 | tf_op jit(solution)/shard_map/psum | solution.py:222
  (193 shorter events, 96.8 us)
Async XLA Ops:
  0.6 30.1 %copy-start.8 = (f32[5,5,1]{1,0,2:T(8,128)S(1)}, f32[5,5,1]{1,0,2:T(8,128)}, u32[]{:S(2)}) copy-start(f32[5,5,1]{1,0,2:T(8,128)} %constant.532) | copy-start | bytes 304
  0.6 30.3 %copy-start.11 = (f32[128,5,1]{0,1,2:T(8,128)S(1)}, f32[128,5,1]{0,1,2:T(8,128)}, u32[]{:S(2)}) copy-start(f32[128,5,1]{0,1,2:T(8,128)} %constant.533) | copy-start | bytes 7684
  2.1 67.6 %collective-permute-start = (f32[5,512]{1,0:T(8,128)S(1)}, f32[5,512]{1,0:T(8,128)S(1)}, u32[]{:S(2)}, u32[]{:S(2)}) collective-permute-start(f32[5,512]{1,0:T(8,128)S(1)} %get-tuple-element.989), channel_id=1, source_target_pairs={{0,1},{1,2},{2,3},{3,4},{4,5},{5,6},{6,7},{7,8},{8,9},{9,10},{10,1... | collective-permute-start | bytes 30728 | tf_op jit(solution)/shard_map/ppermute | solution.py:26
  2.6 67.1 %collective-permute-start.2 = (f32[5,512]{1,0:T(8,128)S(1)}, f32[5,512]{1,0:T(8,128)S(1)}, u32[]{:S(2)}, u32[]{:S(2)}) collective-permute-start(f32[5,512]{1,0:T(8,128)S(1)} %get-tuple-element.990), channel_id=1, source_target_pairs={{1,0},{2,1},{3,2},{4,3},{5,4},{6,5},{7,6},{8,7},{9,8},{10,9},{11,1... | collective-permute-start | bytes 30728 | tf_op jit(solution)/shard_map/ppermute | solution.py:28
  8.6 61.0 %collective-permute-start.1 = (f32[3,512]{1,0:T(4,128)S(1)}, f32[3,512]{1,0:T(4,128)S(1)}, u32[]{:S(2)}, u32[]{:S(2)}) collective-permute-start(f32[3,512]{1,0:T(4,128)S(1)} %get-tuple-element.1085), channel_id=1, source_target_pairs={{0,1},{1,2},{2,3},{3,4},{4,5},{5,6},{6,7},{7,8},{8,9},{9,10},{10,1... | collective-permute-start | bytes 18440 | tf_op jit(solution)/shard_map/ppermute | solution.py:26
  8.6 61.0 %collective-permute-start.3 = (f32[3,512]{1,0:T(4,128)S(1)}, f32[3,512]{1,0:T(4,128)S(1)}, u32[]{:S(2)}, u32[]{:S(2)}) collective-permute-start(f32[3,512]{1,0:T(4,128)S(1)} %get-tuple-element.1086), channel_id=1, source_target_pairs={{1,0},{2,1},{3,2},{4,3},{5,4},{6,5},{7,6},{8,7},{9,8},{10,9},{11,1... | collective-permute-start | bytes 18440 | tf_op jit(solution)/shard_map/ppermute | solution.py:28
  13.1 19.8 %copy-start.10 = (f32[128,5,1]{0,1,2:T(8,128)S(1)}, f32[128,5,1]{0,1,2:T(8,128)}, u32[]{:S(2)}) copy-start(f32[128,5,1]{0,1,2:T(8,128)} %constant.534) | copy-start | bytes 7684
  32.8 1.8 copy-start.9
  36.5 19.2 %copy-start.2 = (f32[128]{0:T(128)S(1)}, f32[128]{0:T(128)}, u32[]{:S(2)}) copy-start(f32[128]{0:T(128)} %constant.2011) | copy-start | bytes 1540
  36.5 19.2 %copy-start.4 = (f32[128]{0:T(128)S(1)}, f32[128]{0:T(128)}, u32[]{:S(2)}) copy-start(f32[128]{0:T(128)} %constant.489.clone..sunk.15) | copy-start | bytes 1540
  36.5 19.2 %copy-start.5 = (f32[128]{0:T(128)S(1)}, f32[128]{0:T(128)}, u32[]{:S(2)}) copy-start(f32[128]{0:T(128)} %constant.2010) | copy-start | bytes 1540
  36.5 19.2 %copy-start.6 = (f32[128]{0:T(128)S(1)}, f32[128]{0:T(128)}, u32[]{:S(2)}) copy-start(f32[128]{0:T(128)} %constant.490.clone..sunk.15) | copy-start | bytes 1540
  36.5 19.2 %copy-start.7 = (f32[128]{0:T(128)S(1)}, f32[128]{0:T(128)}, u32[]{:S(2)}) copy-start(f32[128]{0:T(128)} %constant.2009) | copy-start | bytes 1540
  55.7 13.5 %copy-start = (s32[16,9]{1,0:T(8,128)S(1)}, s32[16,9]{1,0:T(8,128)}, u32[]{:S(2)}) copy-start(s32[16,9]{1,0:T(8,128)} %param.28) | copy-start | bytes 1732
  55.7 13.8 %copy-start.1 = (f32[2048]{0:T(1024)S(1)}, f32[2048]{0:T(1024)}, u32[]{:S(2)}) copy-start(f32[2048]{0:T(1024)} %param.25) | copy-start | bytes 24580
  55.7 14.0 %copy-start.3 = (f32[3,2048]{1,0:T(4,128)S(1)}, f32[3,2048]{1,0:T(4,128)}, u32[]{:S(2)}) copy-start(f32[3,2048]{1,0:T(4,128)} %param.24) | copy-start | bytes 73732
  123.3 35.3 %collective-permute-start.4 = (f32[3,512]{1,0:T(4,128)S(1)}, f32[3,512]{1,0:T(4,128)S(1)}, u32[]{:S(2)}, u32[]{:S(2)}) collective-permute-start(f32[3,512]{1,0:T(4,128)S(1)} %get-tuple-element.1077), channel_id=1, source_target_pairs={{0,1},{1,2},{2,3},{3,4},{4,5},{5,6},{6,7},{7,8},{8,9},{9,10},{10,1... | collective-permute-start | bytes 18440 | tf_op jit(solution)/shard_map/ppermute | solution.py:26
  123.3 35.2 %collective-permute-start.5 = (f32[3,512]{1,0:T(4,128)S(1)}, f32[3,512]{1,0:T(4,128)S(1)}, u32[]{:S(2)}, u32[]{:S(2)}) collective-permute-start(f32[3,512]{1,0:T(4,128)S(1)} %get-tuple-element.1078), channel_id=1, source_target_pairs={{1,0},{2,1},{3,2},{4,3},{5,4},{6,5},{7,6},{8,7},{9,8},{10,9},{11,1... | collective-permute-start | bytes 18440 | tf_op jit(solution)/shard_map/ppermute | solution.py:28
  276.6 35.6 %collective-permute-start.6 = (f32[3,512]{1,0:T(4,128)S(1)}, f32[3,512]{1,0:T(4,128)S(1)}, u32[]{:S(2)}, u32[]{:S(2)}) collective-permute-start(f32[3,512]{1,0:T(4,128)S(1)} %get-tuple-element.1069), channel_id=1, source_target_pairs={{0,1},{1,2},{2,3},{3,4},{4,5},{5,6},{6,7},{7,8},{8,9},{9,10},{10,1... | collective-permute-start | bytes 18440 | tf_op jit(solution)/shard_map/ppermute | solution.py:26
  276.7 35.6 %collective-permute-start.7 = (f32[3,512]{1,0:T(4,128)S(1)}, f32[3,512]{1,0:T(4,128)S(1)}, u32[]{:S(2)}, u32[]{:S(2)}) collective-permute-start(f32[3,512]{1,0:T(4,128)S(1)} %get-tuple-element.1070), channel_id=1, source_target_pairs={{1,0},{2,1},{3,2},{4,3},{5,4},{6,5},{7,6},{8,7},{9,8},{10,9},{11,1... | collective-permute-start | bytes 18440 | tf_op jit(solution)/shard_map/ppermute | solution.py:28
